TPU v7x, 256 devices: a whole 4x4x8 slice. The times are simulated.
256 devices in a mesh: blk: 32 (over y, z), rep: 8 (over x, core).
Axes of the slice: x: 4, y: 4, z: 8, core: 2. Of those that a mesh axis runs over, the one named last changes fastest.
Arguments:
- hidden_in: bfloat16 [8, 512, 2560], P('rep', 'blk'), may hold values from -6 to 6
- w_z: bfloat16 [2560, 4096], P(None, 'blk'), may hold values from -0.125 to 0.125
- w_x: bfloat16 [2560, 4096], P(None, 'blk'), may hold values from -0.125 to 0.125
- w_bc: bfloat16 [2560, 256], replicated, may hold values from -0.125 to 0.125
- w_dt: bfloat16 [2560, 64], P(None, 'blk'), may hold values from -0.125 to 0.125
- conv_x: float32 [4, 4096], P(None, 'blk'), may hold values from -3 to 3
- conv_bc: float32 [4, 256], replicated, may hold values from -3 to 3
- dt_bias: float32 [4, 64], P(None, 'blk'), may hold values from -3 to -0.5
- a_log: float32 [64], P('blk'), may hold values from -2.5 to 0.5
- d_skip: float32 [64], P('blk'), may hold values from 0.5 to 1.5
- norm_gain: float32 [4096], P('blk'), may hold values from 0.5 to 1.5
- w_out: bfloat16 [4096, 2560], P('blk'), may hold values from -0.09375 to 0.09375
- edge_x: bfloat16 [256, 3, 4096], P('rep', None, 'blk'), may hold values from -6 to 6
- edge_bc: bfloat16 [256, 3, 256], P('rep'), may hold values from -6 to 6
- pool: float32 [384, 64, 64, 128], P('rep', 'blk'), may hold values from -0.6 to 0.6
- tenant_sizes: int32 [4], replicated, may hold values from 1 to 128, 256 in all
- owner: int32 [256, 1], P('rep'), may hold values from 0 to 7; in each aligned block of 32 rows (0 to 31, 32 to 63, ...) at most 6 rows name the same one
- accepted: int32 [256], P('rep'), may hold values from 1 to 16
- prompt_len: int32 [256], P('rep'), may hold values from 1 to 11
Outputs:
- hidden_out: bfloat16 [8, 512, 2560], P('rep', 'blk')
- new_pool: float32 [384, 64, 64, 128], P('rep', 'blk')
Inputs may be any that keep to these rules, and one draw needn't show every extreme that they name: Among the requests of one group (aligned blocks of 32 requests) each owner is named at most 6 times, a bound that some block reaches. `tenant_sizes`: the sizes sum to 256.
All inputs are finite; a program needn't handle non-finite values.
Results may differ from a plain program's by a relative error of at most 0.025.
Values may be sent and summed in bfloat16 or wider, within the bound.
A program may use at most 64 MiB of HBM per device.

v0:
```python
import jax
import jax.numpy as jnp
from jax import lax
from jax.sharding import PartitionSpec as P


def convolve(edge_cells, fresh_cells, kernel, edge_mask):
    sequence = jnp.concatenate(
        [edge_cells * edge_mask[:, :, None].astype(edge_cells.dtype), fresh_cells], 1
    ).astype(jnp.float32)
    steps_count = fresh_cells.shape[1]
    summed = kernel[0] * sequence[:, 0:steps_count]
    for offset in range(1, kernel.shape[0]):
        summed = summed + kernel[offset] * sequence[:, offset : offset + steps_count]
    return jax.nn.silu(summed).astype(jnp.bfloat16)


def shards(
    hidden_in,
    w_z,
    w_x,
    w_bc,
    w_dt,
    conv_x,
    conv_bc,
    dt_bias,
    a_log,
    d_skip,
    norm_gain,
    w_out,
    edge_x,
    edge_bc,
    pool,
    tenant_sizes,
    owner,
    accepted,
    prompt_len,
):
    highest = lax.Precision.HIGHEST
    rows_in = hidden_in[0]
    local_rows = rows_in.shape[0]
    n_req = edge_x.shape[0]
    drafts = local_rows * lax.axis_size("blk") // n_req
    state_dim = w_bc.shape[1] // 2
    heads_here = w_dt.shape[1]
    inner_here = w_z.shape[1]
    head_dim = inner_here // heads_here
    slots_here = pool.shape[0]
    cap_group = slots_here // lax.axis_size("rep")
    weights_in = (w_z, w_x, w_dt, w_bc)
    block_rows = lax.all_gather(rows_in, "blk", axis=0, tiled=True)
    projected = jnp.concatenate(
        [
            jnp.dot(block_rows, weight_cols, preferred_element_type=jnp.float32)
            for weight_cols in weights_in
        ],
        1,
    ).astype(jnp.bfloat16)
    z_all = projected[:, :inner_here]
    u_all = projected[:, inner_here : 2 * inner_here]
    dt_raw = projected[:, 2 * inner_here : 2 * inner_here + heads_here]
    bc_all = projected[:, 2 * inner_here + heads_here :]
    edge_len = edge_x.shape[1]
    edge_mask = prompt_len[:, None] >= (edge_len - jnp.arange(edge_len, dtype=jnp.int32))[None, :]
    x_conv = convolve(edge_x, u_all.reshape(n_req, drafts, inner_here), conv_x, edge_mask)
    bc_conv = convolve(edge_bc, bc_all.reshape(n_req, drafts, 2 * state_dim), conv_bc, edge_mask)
    b_half = bc_conv[:, :, :state_dim]
    c_half = bc_conv[:, :, state_dim:]
    b_float = b_half.astype(jnp.float32)
    c_float = c_half.astype(jnp.float32)
    x_heads = x_conv.reshape(n_req, drafts, heads_here, head_dim).astype(jnp.float32)
    req_index = lax.axis_index("rep") * n_req + jnp.arange(n_req, dtype=jnp.int32)
    tenant_ends = jnp.cumsum(tenant_sizes)
    tenant_id = jnp.sum((req_index[:, None] >= tenant_ends[None, :-1]).astype(jnp.int32), axis=1)
    tenant_pick = (
        tenant_id[:, None] == jnp.arange(tenant_sizes.shape[0], dtype=jnp.int32)[None, :]
    ).astype(jnp.float32)
    bias_req = jnp.dot(tenant_pick, dt_bias, precision=highest)
    step_size = jax.nn.softplus(
        dt_raw.reshape(n_req, drafts, heads_here).astype(jnp.float32) + bias_req[:, None, :]
    )
    log_decay = jnp.cumsum(step_size * (-jnp.exp(a_log))[None, None, :], axis=1)
    draft_index = jnp.arange(drafts, dtype=jnp.int32)
    causal = draft_index[:, None] >= draft_index[None, :]
    scores = jnp.einsum("rtn,rsn->rts", c_float, b_float, precision=highest)
    log_gap = log_decay[:, :, None, :] - log_decay[:, None, :, :]
    weight = (
        jnp.where(causal[None, :, :, None], jnp.exp(jnp.minimum(log_gap, 0.0)), 0.0)
        * step_size[:, None, :, :]
        * scores[:, :, :, None]
    )
    y_local = (
        jnp.einsum("rtsh,rshp->rthp", weight, x_heads, precision=highest)
        + d_skip[None, None, :, None] * x_heads
    )
    pick_last = (draft_index[None, :] == accepted[:, None] - 1).astype(jnp.float32)
    log_accept = jnp.sum(pick_last[:, :, None] * log_decay, axis=1)
    keep_draft = draft_index[None, :] < accepted[:, None]
    coef = (
        jnp.where(
            keep_draft[:, :, None],
            jnp.exp(jnp.minimum(log_accept[:, None, :] - log_decay, 0.0)),
            0.0,
        )
        * step_size
    )
    carry_decay = jnp.exp(log_accept)
    decay_now = jnp.exp(log_decay)
    owner_of = owner[:, 0]
    local_index = jnp.arange(n_req, dtype=jnp.int32)
    earlier = (owner_of[None, :] == owner_of[:, None]) & (
        local_index[None, :] < local_index[:, None]
    )
    rank_within = jnp.sum(earlier.astype(jnp.int32), axis=1)
    slot_index = owner_of * cap_group + rank_within
    fetched = lax.all_to_all(
        pool.astype(jnp.bfloat16), "rep", split_axis=0, concat_axis=0, tiled=True
    ).astype(pool.dtype)
    start_state = jnp.take(fetched, slot_index, axis=0)
    y_prior = decay_now[:, :, :, None] * jnp.einsum(
        "rhpn,rtn->rthp", start_state, c_float, precision=highest
    )
    accepted_state = carry_decay[:, :, None, None] * start_state + jnp.einsum(
        "rsh,rshp,rsn->rhpn", coef, x_heads, b_float, precision=highest
    )
    buffer = jnp.zeros(pool.shape, jnp.float32).at[slot_index].set(accepted_state)
    new_pool = lax.all_to_all(
        buffer.astype(jnp.bfloat16), "rep", split_axis=0, concat_axis=0, tiled=True
    ).astype(buffer.dtype)
    y_total = (y_local + y_prior).reshape(n_req * drafts, inner_here)
    gated = y_total * jax.nn.silu(z_all.astype(jnp.float32))
    sq_total = lax.psum(jnp.sum(gated * gated, axis=1), "blk")
    inner_all = inner_here * lax.axis_size("blk")
    normed = (gated * lax.rsqrt(sq_total / inner_all + 1e-05)[:, None] * norm_gain[None, :]).astype(
        jnp.bfloat16
    )
    block_rows = normed
    mixed = lax.psum_scatter(
        jnp.dot(block_rows, w_out, preferred_element_type=jnp.float32).astype(jnp.bfloat16),
        "blk",
        scatter_dimension=0,
        tiled=True,
    )
    return (mixed[None], new_pool)


def solution(mesh):
    placed = (
        P("rep", "blk", None),
        P(None, "blk"),
        P(None, "blk"),
        P(),
        P(None, "blk"),
        P(None, "blk"),
        P(),
        P(None, "blk"),
        P("blk"),
        P("blk"),
        P("blk"),
        P("blk", None),
        P("rep", None, "blk"),
        P("rep", None, None),
        P("rep", "blk", None, None),
        P(),
        P("rep", None),
        P("rep"),
        P("rep"),
    )
    return jax.shard_map(
        shards,
        mesh=mesh,
        in_specs=placed,
        out_specs=(P("rep", "blk", None), P("rep", "blk", None, None)),
        check_vma=False,
    )
```

profile of v0, /device:TPU:2, one launch (start us, length us, event | category | flops | bytes accessed | tf_op | source)
XLA Modules:
  0.0 418.3 jit_solution(11525417549869949106)
XLA Ops:
  7.9 3.4 convert_element_type.82
  11.4 5.9 %all-to-all-start = ((bf16[48,2,64,128]{3,2,1,0:T(8,128)(2,1)}), bf16[48,2,64,128]{3,2,1,0:T(8,128)(2,1)S(1)}, u32[]{:S(2)}, u32[]{:S(2)}) async-start(bf16[48,2,64,128]{3,2,1,0:T(8,128)(2,1)} %convert_element_type.82), calls=%async_computation | async-start | bytes 3145728 | tf_op jit(solution)/shard_map/all_to_all | solution.py:116
  22.3 0.7 copy_multiply_fusion
  23.0 14.5 %all-to-all-done = bf16[48,2,64,128]{3,2,1,0:T(8,128)(2,1)S(1)} async-done(((bf16[48,2,64,128]{3,2,1,0:T(8,128)(2,1)}), bf16[48,2,64,128]{3,2,1,0:T(8,128)(2,1)S(1)}, u32[]{:S(2)}, u32[]{:S(2)}) %all-to-all-start) | async-done | bytes 1572896 | tf_op jit(solution)/shard_map/all_to_all | solution.py:116
  37.5 2.1 convert_element_type.83
  39.5 2.6 gather_fusion
  42.1 50.4 %all-gather.3.cloned.1.call-done = bf16[1,512,2560]{2,1,0:T(8,128)(2,1)} async-done(((bf16[1,16,2560]{2,1,0:T(8,128)(2,1)}), bf16[1,512,2560]{2,1,0:T(8,128)(2,1)}) %all-gather.3.cloned.1.call-update) | async-done | bytes 2621456 | tf_op jit(solution)/shard_map/all_gather | solution.py:51
  92.5 2.5 fusion.32
  95.2 0.7 broadcast_multiply_fusion.1
  96.6 2.7 fusion.20
  99.6 0.9 reshape.167
  100.5 1.6 copy.77
  102.0 1.7 fusion.76
  103.7 1.2 copy.78
  104.9 1.7 multiply_reduce_fusion
  106.7 1.2 copy.85
  107.9 2.6 fusion.17
  112.1 2.6 fusion.13
  114.8 1.1 copy.86
  115.8 2.0 reshape.170
  117.9 1.8 copy.87
  119.7 3.7 multiply_reduce_fusion.1
  123.4 72.2 %psum.7 = f32[512]{0:T(512)S(1)} all-reduce(f32[512]{0:T(512)S(1)} %get-tuple-element.16), channel_id=1, replica_groups=mesh['blk'=32,'rep'=8] {'blk'}, use_global_device_ids=true, to_apply=%region_5.6 | all-reduce | flops 512 | bytes 4096 | tf_op jit(solution)/shard_map/psum | solution.py:132
  195.6 3.6 convolution_convert_fusion
  199.9 1.1 copy.89
  201.2 4.6 %multiply_add_fusion = f32[32,2,64,128]{3,2,1,0:T(8,128)} fusion(f32[32,2,64,128]{3,2,1,0:T(8,128)S(1)} %gather_fusion, f32[32,2]{1,0:T(8,128)S(1)} %exp.50, pred[32]{0:T(512)(128)(4,1)S(1)} %copy-done.12, f32[32,16,2]{1,2,0:T(2,128)S(1)} %copy.90, bf16[32,16,2,64]{3,2,1,0:T(2,128)(2,1)} %reshape.167, bf16[32,16,256]{2,1,0:T(8,128)(2,1)} %copy-done.2), kind=kOutput, calls=%fused_computation.11 | convolution fusion | flops 102367232 | bytes 4591904 | tf_op jit(solution)/shard_map/rsh,rshp,rsn->rhpn/dot_general | solution.py:123
  205.7 2.1 broadcast_in_dim.31
  207.9 5.3 %scatter_fusion = f32[48,2,64,128]{3,2,1,0:T(8,128)} fusion(f32[48,2,64,128]{3,2,1,0:T(8,128)} %broadcast_in_dim.31, s32[32]{0:T(128)S(1)} %bitcast.79, f32[32,2,64,128]{3,2,1,0:T(8,128)S(1)} %copy-done.1), kind=kCustom, calls=%fused_computation.1 | custom fusion | bytes 6291584 | tf_op jit(solution)/shard_map/scatter | solution.py:126
  213.2 2.3 convert_element_type.88
  215.5 24.9 %all_to_all.10 = bf16[48,2,64,128]{3,2,1,0:T(8,128)(2,1)S(1)} all-to-all(bf16[48,2,64,128]{3,2,1,0:T(8,128)(2,1)S(1)} %convert_element_type.88), channel_id=1, replica_groups=mesh['blk'=32,'rep'=8] {'rep'}, dimensions={0} | all-to-all | bytes 3145728 | tf_op jit(solution)/shard_map/all_to_all | solution.py:127
  240.4 2.0 convert_element_type.89
  242.5 169.0 %reduce-scatter.2.cloned.1.call-done = bf16[16,2560]{1,0:T(8,128)(2,1)} async-done(((bf16[512,2560]{1,0:T(8,128)(2,1)}), bf16[16,2560]{1,0:T(8,128)(2,1)}) %reduce-scatter.2.cloned.1.call-update) | async-done | bytes 81936 | tf_op jit(solution)/shard_map/reduce_scatter | solution.py:138
  (104 shorter events, 9.2 us)
Async XLA Ops:
  7.2 100.7 %copy-start = (bf16[2560,256]{1,0:T(8,128)(2,1)S(1)}, bf16[2560,256]{1,0:T(8,128)(2,1)}, u32[]{:S(2)}) copy-start(bf16[2560,256]{1,0:T(8,128)(2,1)} %param.22) | copy-start | bytes 3932164
  7.2 85.3 %all-gather.3.cloned.1.call-start = ((), (), s32[]{:S(2)}) async-start(), calls=%async_computation.4 | async-start | bytes 2703360 | tf_op jit(solution)/shard_map/all_gather | solution.py:51
  11.3 6.0 %copy-start.30 = (s32[4]{0:T(128)S(1)}, s32[4]{0:T(128)}, u32[]{:S(2)}) copy-start(s32[4]{0:T(128)} %param.34) | copy-start | bytes 52
  11.3 6.2 %copy-start.27 = (s32[32,1]{0,1:T(1,128)S(1)}, s32[32,1]{0,1:T(1,128)}, u32[]{:S(2)}) copy-start(s32[32,1]{0,1:T(1,128)} %param.35) | copy-start | bytes 388
  11.3 7.0 %copy-start.31 = (f32[2]{0:T(128)S(1)}, f32[2]{0:T(128)}, u32[]{:S(2)}) copy-start(f32[2]{0:T(128)} %param.27) | copy-start | bytes 28
  11.3 7.5 %copy-start.28 = (s32[32]{0:T(128)S(1)}, s32[32]{0:T(128)}, u32[]{:S(2)}) copy-start(s32[32]{0:T(128)} %param.37) | copy-start | bytes 388
  11.3 7.5 %copy-start.8 = (bf16[32,3,128]{2,0,1:T(8,128)(2,1)S(1)}, bf16[32,3,128]{2,0,1:T(8,128)(2,1)}, u32[]{:S(2)}) copy-start(bf16[32,3,128]{2,0,1:T(8,128)(2,1)} %param.31) | copy-start | bytes 73732
  11.4 8.9 %copy-start.25 = (s32[32]{0:T(128)S(1)}, s32[32]{0:T(128)}, u32[]{:S(2)}) copy-start(s32[32]{0:T(128)} %param.36) | copy-start | bytes 388
  11.4 8.9 %copy-start.29 = (f32[4,2]{0,1:T(2,128)S(1)}, f32[4,2]{0,1:T(2,128)}, u32[]{:S(2)}) copy-start(f32[4,2]{0,1:T(2,128)} %param.26) | copy-start | bytes 100
  11.4 9.1 %copy-start.22 = (f32[4,128]{1,0:T(4,128)S(1)}, f32[4,128]{1,0:T(4,128)}, u32[]{:S(2)}) copy-start(f32[4,128]{1,0:T(4,128)} %param.24) | copy-start | bytes 6148
  11.4 9.7 %copy-start.17 = (f32[4,256]{1,0:T(4,128)S(1)}, f32[4,256]{1,0:T(4,128)}, u32[]{:S(2)}) copy-start(f32[4,256]{1,0:T(4,128)} %param.25) | copy-start | bytes 12292
  11.4 10.8 %copy-start.6 = (bf16[32,3,256]{2,0,1:T(8,128)(2,1)S(1)}, bf16[32,3,256]{2,0,1:T(8,128)(2,1)}, u32[]{:S(2)}) copy-start(bf16[32,3,256]{2,0,1:T(8,128)(2,1)} %param.32) | copy-start | bytes 147460
  11.4 26.1 %all-to-all-start = ((bf16[48,2,64,128]{3,2,1,0:T(8,128)(2,1)}), bf16[48,2,64,128]{3,2,1,0:T(8,128)(2,1)S(1)}, u32[]{:S(2)}, u32[]{:S(2)}) async-start(bf16[48,2,64,128]{3,2,1,0:T(8,128)(2,1)} %convert_element_type.82), calls=%async_computation | async-start | bytes 3145728 | tf_op jit(solution)/shard_map/all_to_all | solution.py:116
  17.3 394.1 %reduce-scatter.2.cloned.1.call-start = ((), (), s32[]{:S(2)}) async-start(), calls=%async_computation.3 | async-start | bytes 2703360 | tf_op jit(solution)/shard_map/reduce_scatter | solution.py:138
  39.5 53.0 %copy-start.9 = (bf16[2560,2]{0,1:T(2,128)(2,1)S(1)}, bf16[2560,2]{0,1:T(2,128)(2,1)}, u32[]{:S(2)}) copy-start(bf16[2560,2]{0,1:T(2,128)(2,1)} %param.23) | copy-start | bytes 30724
  96.6 2.8 copy-start.5
  96.6 2.8 copy-start.18
  96.6 2.8 copy-start.19
  96.6 2.8 copy-start.20
  96.6 2.8 copy-start.21
  107.9 2.7 copy-start.4
  107.9 2.8 copy-start.13
  107.9 2.8 copy-start.14
  107.9 2.8 copy-start.15
  107.9 2.8 copy-start.16
  110.5 1.0 copy-start.3
  110.5 0.9 copy-start.7
  110.7 1.4 copy-start.12
  111.1 3.7 copy-start.2
  119.7 75.9 %copy-start.24 = (f32[128]{0:T(128)S(1)}, f32[128]{0:T(128)}, u32[]{:S(2)}) copy-start(f32[128]{0:T(128)} %param.29) | copy-start | bytes 1540
  205.7 2.1 copy-start.1
  205.7 2.1 copy-start.11
  (4 other events, 3.1 us)
Sparse Core Ops, SparseCore 0:
  10.6 81.8 all-gather.2
  199.3 212.0 reduce-scatter.1
where the time goes:
time: 419 us; the launch traced here: 418 us
  waiting for transfers between devices  235 us (56%)
  blocking collectives  97.1 us (23%)
  local copies, waits for them, and re-layouts  25.3 us (6%)
  matrix products  23.3 us (6%)
  other arithmetic  17.6 us (4%)
  between operations  14.4 us (3%)
  starting transfers between devices  5.94 us (1%)
    reduce_scatter x1, waiting for transfers between devices, shards(): lax.psum_scatter(jnp.dot(block_rows, w_out, preferred_element_type=jnp.fl...  169 us
    psum x1, blocking collectives, shards(): sq_total = lax.psum(jnp.sum(gated * gated, axis=1), 'blk')  72.2 us
    all_gather x1, waiting for transfers between devices, shards(): block_rows = lax.all_gather(rows_in, 'blk', axis=0, tiled=True)  50.4 us
    all_to_all x1, blocking collectives, shards(): lax.all_to_all(buffer.astype(jnp.bfloat16), 'rep', split_axis=0, concat_a...  24.9 us
    all_to_all x1, waiting for transfers between devices, shards(): lax.all_to_all(pool.astype(jnp.bfloat16), 'rep', split_axis=0, concat_axi...  14.5 us
    dot_general x4, matrix products, shards(): jnp.dot(block_rows, weight_cols, preferred_element_type=jnp.float32)  11.5 us
  transfers between devices with their start and end apart: 3, of which 3 were waited for; matrix products, arithmetic and copies ran while one was open for 7% of the time, Pallas kernels for 0%

commit v1 on v0

--- a/solution.py
+++ b/solution.py
@@ -48,7 +48,9 @@
     slots_here = pool.shape[0]
     cap_group = slots_here // lax.axis_size("rep")
     weights_in = (w_z, w_x, w_dt, w_bc)
-    block_rows = lax.all_gather(rows_in, "blk", axis=0, tiled=True)
+    block_rows = jnp.concatenate(
+        lax.all_to_all(jnp.stack([rows_in] * lax.axis_size("blk")), "blk", 0, 0), axis=0
+    )
     projected = jnp.concatenate(
         [
             jnp.dot(block_rows, weight_cols, preferred_element_type=jnp.float32)

time: 419 us -> 436 us (1.041)
  blocking collectives: 97.1 us -> 120 us
  waiting for transfers between devices: 235 us -> 223 us
  starting transfers between devices: 5.94 us -> 11.7 us
    all_gather x1 -> x0, waiting for transfers between devices: 50.4 us -> none  [shards(): block_rows = lax.all_gather(rows_in, 'blk', axis=0, tiled=True)]
    all_to_all x1, waiting for transfers between devices: 14.5 us -> 53 us  [shards(): lax.all_to_all(jnp.stack([rows_in] * lax.axis_size('blk')), 'blk', 0, 0)]
    all_to_all x0 -> x1, blocking collectives: none -> 25.2 us  [shards(): lax.all_to_all(pool.astype(jnp.bfloat16), 'rep', split_axis=0, concat_axi...]
    all_to_all x1, starting transfers between devices: 5.9 us -> 11.7 us  [shards(): lax.all_to_all(jnp.stack([rows_in] * lax.axis_size('blk')), 'blk', 0, 0)]
  transfers between devices with their start and end apart: 3 -> 2, of which waited for: 3 -> 2; matrix products, arithmetic and copies ran while one was open for 7% -> 6% of each run, Pallas kernels for 0% -> 0%
where the time goes in v1:
time: 436 us; the launch traced here: 435 us
  waiting for transfers between devices  223 us (51%)
  blocking collectives  120 us (28%)
  local copies, waits for them, and re-layouts  26.7 us (6%)
  matrix products  23.3 us (5%)
  other arithmetic  16.6 us (4%)
  between operations  14.5 us (3%)
  starting transfers between devices  11.7 us (3%)
    reduce_scatter x1, waiting for transfers between devices, shards(): lax.psum_scatter(jnp.dot(block_rows, w_out, preferred_element_type=jnp.fl...  170 us
    psum x1, blocking collectives, shards(): sq_total = lax.psum(jnp.sum(gated * gated, axis=1), 'blk')  70.2 us
    all_to_all x1, waiting for transfers between devices, shards(): lax.all_to_all(jnp.stack([rows_in] * lax.axis_size('blk')), 'blk', 0, 0)  53 us
    all_to_all x1, blocking collectives, shards(): lax.all_to_all(pool.astype(jnp.bfloat16), 'rep', split_axis=0, concat_axi...  25.2 us
    all_to_all x1, blocking collectives, shards(): lax.all_to_all(buffer.astype(jnp.bfloat16), 'rep', split_axis=0, concat_a...  24.3 us
    all_to_all x1, starting transfers between devices, shards(): lax.all_to_all(jnp.stack([rows_in] * lax.axis_size('blk')), 'blk', 0, 0)  11.7 us
    dot_general x4, matrix products, shards(): jnp.dot(block_rows, weight_cols, preferred_element_type=jnp.float32)  11.5 us
  transfers between devices with their start and end apart: 2, of which 2 were waited for; matrix products, arithmetic and copies ran while one was open for 6% of the time, Pallas kernels for 0%

profile of v1, /device:TPU:2, one launch (start us, length us, event | category | flops | bytes accessed | tf_op | source)
XLA Modules:
  0.0 435.1 jit_solution(17296472975033430649)
XLA Ops:
  7.2 2.4 convert_element_type.82
  9.6 25.2 %all_to_all.15 = bf16[48,2,64,128]{3,2,1,0:T(8,128)(2,1)S(1)} all-to-all(bf16[48,2,64,128]{3,2,1,0:T(8,128)(2,1)S(1)} %convert_element_type.82), channel_id=1, replica_groups=mesh['blk'=32,'rep'=8] {'rep'}, dimensions={0} | all-to-all | bytes 3145728 | tf_op jit(solution)/shard_map/all_to_all | solution.py:118
  34.7 1.8 stack.3
  36.6 11.7 %all-to-all-start = ((bf16[32,16,2560]{2,1,0:T(8,128)(2,1)}), bf16[32,16,2560]{2,1,0:T(8,128)(2,1)}, u32[]{:S(2)}, u32[]{:S(2)}) async-start(bf16[32,16,2560]{2,1,0:T(8,128)(2,1)} %stack.3), calls=%async_computation | async-start | bytes 5242880 | tf_op jit(solution)/shard_map/all_to_all | solution.py:52
  53.0 0.7 copy_multiply_fusion
  53.7 2.1 convert_element_type.83
  55.8 2.6 gather_fusion
  58.4 53.0 %all-to-all-done = bf16[32,16,2560]{2,1,0:T(8,128)(2,1)} async-done(((bf16[32,16,2560]{2,1,0:T(8,128)(2,1)}), bf16[32,16,2560]{2,1,0:T(8,128)(2,1)}, u32[]{:S(2)}, u32[]{:S(2)}) %all-to-all-start) | async-done | bytes 2621472 | tf_op jit(solution)/shard_map/all_to_all | solution.py:52
  111.3 2.5 fusion.10
  115.4 2.7 convolution_convert_fusion.3
  118.4 0.9 reshape.172
  119.3 1.6 copy.77
  120.9 1.7 fusion.50
  122.6 1.2 copy.78
  123.8 1.7 multiply_reduce_fusion
  125.5 1.2 copy.85
  126.8 2.6 convolution_convert_fusion.1
  130.9 2.6 fusion.5
  133.6 1.1 copy.86
  134.7 2.0 reshape.175
  136.7 1.8 copy.87
  138.5 3.7 multiply_reduce_fusion.1
  142.2 70.2 %psum.7 = f32[512]{0:T(512)S(1)} all-reduce(f32[512]{0:T(512)S(1)} %get-tuple-element.16), channel_id=1, replica_groups=mesh['blk'=32,'rep'=8] {'blk'}, use_global_device_ids=true, to_apply=%region_5.6 | all-reduce | flops 512 | bytes 4096 | tf_op jit(solution)/shard_map/psum | solution.py:134
  212.5 3.6 convolution_convert_fusion
  216.7 1.1 copy.89
  218.0 4.5 %multiply_add_fusion = f32[32,2,64,128]{3,2,1,0:T(8,128)} fusion(f32[32,2,64,128]{3,2,1,0:T(8,128)S(1)} %gather_fusion, f32[32,2]{1,0:T(8,128)S(1)} %exp.50, pred[32]{0:T(512)(128)(4,1)S(1)} %copy-done.13, f32[32,16,2]{1,2,0:T(2,128)S(1)} %copy.90, bf16[32,16,2,64]{3,2,1,0:T(2,128)(2,1)} %reshape.172, bf16[32,16,256]{2,1,0:T(8,128)(2,1)} %copy-done.2), kind=kOutput, calls=%fused_computation.3 | convolution fusion | flops 102367232 | bytes 4591904 | tf_op jit(solution)/shard_map/rsh,rshp,rsn->rhpn/dot_general | solution.py:125
  222.6 2.1 broadcast_in_dim.31
  224.7 5.4 %scatter_fusion = f32[48,2,64,128]{3,2,1,0:T(8,128)} fusion(f32[48,2,64,128]{3,2,1,0:T(8,128)} %broadcast_in_dim.31, s32[32]{0:T(128)S(1)} %bitcast.61, f32[32,2,64,128]{3,2,1,0:T(8,128)S(1)} %copy-done.1), kind=kCustom, calls=%fused_computation.1 | custom fusion | bytes 6291584 | tf_op jit(solution)/shard_map/scatter | solution.py:128
  230.1 2.2 convert_element_type.88
  232.3 24.3 %all_to_all.16 = bf16[48,2,64,128]{3,2,1,0:T(8,128)(2,1)S(1)} all-to-all(bf16[48,2,64,128]{3,2,1,0:T(8,128)(2,1)S(1)} %convert_element_type.88), channel_id=1, replica_groups=mesh['blk'=32,'rep'=8] {'rep'}, dimensions={0} | all-to-all | bytes 3145728 | tf_op jit(solution)/shard_map/all_to_all | solution.py:129
  256.6 2.0 convert_element_type.89
  258.6 169.6 %reduce-scatter.2.cloned.1.call-done = bf16[16,2560]{1,0:T(8,128)(2,1)} async-done(((bf16[512,2560]{1,0:T(8,128)(2,1)}), bf16[16,2560]{1,0:T(8,128)(2,1)}) %reduce-scatter.2.cloned.1.call-update) | async-done | bytes 81936 | tf_op jit(solution)/shard_map/reduce_scatter | solution.py:140
  (105 shorter events, 8.8 us)
Async XLA Ops:
  7.2 119.6 %copy-start = (bf16[2560,256]{1,0:T(8,128)(2,1)S(1)}, bf16[2560,256]{1,0:T(8,128)(2,1)}, u32[]{:S(2)}) copy-start(bf16[2560,256]{1,0:T(8,128)(2,1)} %param.22) | copy-start | bytes 3932164
  9.5 25.2 %copy-start.6 = (bf16[1,16,2560]{2,1,0:T(8,128)(2,1)S(1)}, bf16[1,16,2560]{2,1,0:T(8,128)(2,1)}, u32[]{:S(2)}) copy-start(bf16[1,16,2560]{2,1,0:T(8,128)(2,1)} %param.19) | copy-start | bytes 245764
  36.6 11.8 %copy-start.28 = (s32[32]{0:T(128)S(1)}, s32[32]{0:T(128)}, u32[]{:S(2)}) copy-start(s32[32]{0:T(128)} %param.37) | copy-start | bytes 388
  36.6 12.0 %copy-start.9 = (bf16[32,3,128]{2,0,1:T(8,128)(2,1)S(1)}, bf16[32,3,128]{2,0,1:T(8,128)(2,1)}, u32[]{:S(2)}) copy-start(bf16[32,3,128]{2,0,1:T(8,128)(2,1)} %param.31) | copy-start | bytes 73732
  36.6 12.7 %copy-start.31 = (s32[4]{0:T(128)S(1)}, s32[4]{0:T(128)}, u32[]{:S(2)}) copy-start(s32[4]{0:T(128)} %param.34) | copy-start | bytes 52
  36.6 13.5 %copy-start.29 = (s32[32,1]{0,1:T(1,128)S(1)}, s32[32,1]{0,1:T(1,128)}, u32[]{:S(2)}) copy-start(s32[32,1]{0,1:T(1,128)} %param.35) | copy-start | bytes 388
  36.6 14.4 %copy-start.32 = (f32[2]{0:T(128)S(1)}, f32[2]{0:T(128)}, u32[]{:S(2)}) copy-start(f32[2]{0:T(128)} %param.27) | copy-start | bytes 28
  36.6 14.4 %copy-start.26 = (s32[32]{0:T(128)S(1)}, s32[32]{0:T(128)}, u32[]{:S(2)}) copy-start(s32[32]{0:T(128)} %param.36) | copy-start | bytes 388
  36.6 14.4 %copy-start.30 = (f32[4,2]{0,1:T(2,128)S(1)}, f32[4,2]{0,1:T(2,128)}, u32[]{:S(2)}) copy-start(f32[4,2]{0,1:T(2,128)} %param.26) | copy-start | bytes 100
  36.6 14.5 %copy-start.23 = (f32[4,128]{1,0:T(4,128)S(1)}, f32[4,128]{1,0:T(4,128)}, u32[]{:S(2)}) copy-start(f32[4,128]{1,0:T(4,128)} %param.24) | copy-start | bytes 6148
  36.6 15.2 %copy-start.18 = (f32[4,256]{1,0:T(4,128)S(1)}, f32[4,256]{1,0:T(4,128)}, u32[]{:S(2)}) copy-start(f32[4,256]{1,0:T(4,128)} %param.25) | copy-start | bytes 12292
  36.6 16.4 %copy-start.7 = (bf16[32,3,256]{2,0,1:T(8,128)(2,1)S(1)}, bf16[32,3,256]{2,0,1:T(8,128)(2,1)}, u32[]{:S(2)}) copy-start(bf16[32,3,256]{2,0,1:T(8,128)(2,1)} %param.32) | copy-start | bytes 147460
  36.6 74.7 %all-to-all-start = ((bf16[32,16,2560]{2,1,0:T(8,128)(2,1)}), bf16[32,16,2560]{2,1,0:T(8,128)(2,1)}, u32[]{:S(2)}, u32[]{:S(2)}) async-start(bf16[32,16,2560]{2,1,0:T(8,128)(2,1)} %stack.3), calls=%async_computation | async-start | bytes 5242880 | tf_op jit(solution)/shard_map/all_to_all | solution.py:52
  48.3 379.9 %reduce-scatter.2.cloned.1.call-start = ((), (), s32[]{:S(2)}) async-start(), calls=%async_computation.4 | async-start | bytes 2703360 | tf_op jit(solution)/shard_map/reduce_scatter | solution.py:140
  50.8 2.9 copy-start.11
  55.8 55.5 %copy-start.10 = (bf16[2560,2]{0,1:T(2,128)(2,1)S(1)}, bf16[2560,2]{0,1:T(2,128)(2,1)}, u32[]{:S(2)}) copy-start(bf16[2560,2]{0,1:T(2,128)(2,1)} %param.23) | copy-start | bytes 30724
  115.4 2.8 copy-start.5
  115.4 2.8 copy-start.19
  115.4 2.8 copy-start.20
  115.4 2.8 copy-start.21
  115.4 2.8 copy-start.22
  126.7 2.7 copy-start.4
  126.7 2.8 copy-start.14
  126.7 2.8 copy-start.15
  126.8 2.8 copy-start.16
  126.8 2.8 copy-start.17
  129.4 1.0 copy-start.3
  129.6 1.4 copy-start.13
  129.9 3.7 copy-start.2
  138.5 74.0 %copy-start.25 = (f32[128]{0:T(128)S(1)}, f32[128]{0:T(128)}, u32[]{:S(2)}) copy-start(f32[128]{0:T(128)} %param.29) | copy-start | bytes 1540
  222.6 2.1 copy-start.1
  222.6 2.1 copy-start.12
  (4 other events, 3.5 us)
Sparse Core Ops, SparseCore 0:
  216.2 211.9 reduce-scatter.1
